TPU v7x, 32 devices: a whole 2x2x4 slice. The times are simulated.
32 devices in a mesh: layer: 2 (over x), row: 4 (over z), col: 4 (over y, core).
Axes of the slice: x: 2, y: 2, z: 4, core: 2. Of those that a mesh axis runs over, the one named last changes fastest.
Arguments:
- query_weight: bfloat16 [32768, 16384], P(('layer', 'row'), 'col'), parts along dimension 0, may hold values from -0.046875 to 0.046875
- sign_input: int32 [32768], P(('layer', 'col')), parts along dimension 0, may hold values from -1 to 1, as said below
- sign_output: int32 [32768], P(('layer', 'row')), parts along dimension 0, may hold values from -1 to 1, as said below
- clip_level: int32 [256, 128], P(('layer', 'row'), 'col'), parts along dimension 0, may hold values from 1 to 8
- calibration: bfloat16 [768, 16384], P(('layer', 'row'), 'col'), parts along dimension 0, may hold values from -6 to 6
Outputs:
- projected: bfloat16 [768, 16384], P(('layer', 'col'), 'row'), parts along dimension 0
There are 2 independent parts, one for each index of `layer`. A program takes and returns all parts, laid end to end along the dimension named above; each array names one. Nothing has to cross between parts.
Inputs may be any that keep to these rules, and one draw needn't show every extreme that they name: `sign_input`: every entry is -1 or 1. `sign_output`: every entry is -1 or 1.
All inputs are finite; a program needn't handle non-finite values.
Results may differ from a plain program's by a relative error of at most 0.0064.
Values may be sent and summed in bfloat16 or wider, within the bound.
A program may use at most 256 MiB of HBM per device.

v0:
```python
import jax
import jax.numpy as jnp
from jax import lax
from jax.sharding import PartitionSpec as P

INNER = 1024
D = 16384
BLK = 128


def sylvester(length):
    indices = jnp.arange(length, dtype=jnp.int32)
    common_bits = indices[:, None] & indices[None, :]
    parity_sum = jnp.zeros((length, length), jnp.int32)
    for bit_number in range(max(length.bit_length() - 1, 1)):
        parity_sum = parity_sum ^ common_bits >> bit_number & 1
    return (1 - 2 * parity_sum).astype(jnp.float32)


def inner_right(weights, sign_vector, inner_size):
    row_total, col_total = weights.shape
    groups = inner_size // 128
    lane_table = jnp.asarray(sylvester(128), jnp.bfloat16)
    mixing = jnp.asarray(sylvester(groups), jnp.float32)
    signed = weights * sign_vector.astype(jnp.bfloat16)[None, :]
    shaped = signed.reshape(row_total, col_total // inner_size, groups, 128)
    partial_sum = jnp.einsum(
        "rage,ef->ragf", shaped, lane_table, preferred_element_type=jnp.float32
    )
    mixed = jnp.einsum("gh,rahf->ragf", mixing, partial_sum, precision=lax.Precision.HIGHEST)
    return mixed.reshape(row_total, col_total).astype(jnp.bfloat16)


def inner_left(weights, sign_vector, inner_size):
    row_total, col_total = weights.shape
    groups = inner_size // 128
    lane_table = jnp.asarray(sylvester(128), jnp.bfloat16)
    mixing = jnp.asarray(sylvester(groups), jnp.float32)
    signed = weights * sign_vector.astype(jnp.bfloat16)[:, None]
    shaped = signed.reshape(row_total // inner_size, groups, 128, col_total)
    partial_sum = jnp.einsum(
        "ef,cgek->cgfk", lane_table, shaped, preferred_element_type=jnp.float32
    )
    mixed = jnp.einsum("gh,chfk->cgfk", mixing, partial_sum, precision=lax.Precision.HIGHEST)
    return mixed.reshape(row_total, col_total).astype(jnp.bfloat16)


def outer_rotate(regrouped, row_count, col_count, out_blocks, in_blocks):
    outer_table = sylvester(row_count * out_blocks)
    rows_table = jnp.asarray(
        outer_table.reshape(row_count, out_blocks, row_count, out_blocks), jnp.bfloat16
    )
    cols_table = jnp.asarray(
        outer_table.reshape(col_count, in_blocks, col_count, in_blocks), jnp.float32
    )
    first_mix = jnp.einsum(
        "sltj,tqjdm->sqldm", rows_table, regrouped, preferred_element_type=jnp.float32
    )
    spread = first_mix.reshape(
        row_count, col_count, out_blocks, first_mix.shape[3], in_blocks, INNER
    )
    second = jnp.einsum("uvqk,sqldkb->suldvb", cols_table, spread, precision=lax.Precision.HIGHEST)
    return (second / D).astype(jnp.bfloat16)


def shards(query_weight, sign_input, sign_output, clip_level, calibration):
    rows_local, cols_local = query_weight.shape
    row_count = lax.axis_size("row")
    col_count = lax.axis_size("col")
    grid_devices = row_count * col_count
    out_blocks = rows_local // INNER
    in_blocks = cols_local // INNER
    piece_rows = INNER // grid_devices
    right_done = inner_right(query_weight, sign_input, INNER)
    both_done = inner_left(right_done, sign_output, INNER)
    shaped = both_done.reshape(1, out_blocks, grid_devices, piece_rows, cols_local)
    regrouped = lax.all_to_all(shaped, ("row", "col"), split_axis=2, concat_axis=0, tiled=True)
    regrouped = regrouped.reshape(row_count, col_count, out_blocks, piece_rows, cols_local)
    rotated = outer_rotate(regrouped, row_count, col_count, out_blocks, in_blocks)
    outgoing = rotated.reshape(grid_devices, out_blocks, 1, piece_rows, cols_local)
    restored = lax.all_to_all(outgoing, ("row", "col"), split_axis=0, concat_axis=2, tiled=True)
    rotated_tile = restored.reshape(rows_local, cols_local)
    level_rows, level_cols = clip_level.shape
    limits = (clip_level.astype(jnp.float32) / 512.0).astype(jnp.bfloat16)
    blocked = rotated_tile.reshape(level_rows, BLK, level_cols, BLK)
    limit_grid = limits[:, None, :, None]
    clipped = jnp.clip(blocked, -limit_grid, limit_grid).reshape(rows_local, cols_local)
    partial_out = lax.dot_general(
        lax.all_gather(calibration, "row", axis=0, tiled=True),
        clipped,
        (((1,), (1,)), ((), ())),
        preferred_element_type=jnp.float32,
    )
    summed = lax.psum_scatter(partial_out, "col", scatter_dimension=0, tiled=True)
    return summed.astype(jnp.bfloat16)


def solution(mesh):
    placed = (
        P(("layer", "row"), "col"),
        P(("layer", "col")),
        P(("layer", "row")),
        P(("layer", "row"), "col"),
        P(("layer", "row"), "col"),
    )
    return jax.shard_map(
        shards, mesh=mesh, in_specs=placed, out_specs=P(("layer", "col"), "row"), check_vma=False
    )
```

profile of v0, /device:TPU:0, one launch (start us, length us, event | category | flops | bytes accessed | tf_op | source)
XLA Modules:
  0.0 2466.3 jit_solution(11451322066185944695)
XLA Ops:
  6.5 0.7 convert_element_type.76
  7.3 23.3 multiply_bitcast_fusion
  30.5 23.1 copy.62
  53.6 33.6 %fusion.31 = f32[4096,4,8,128]{3,2,1,0:T(8,128)} fusion(bf16[4096,4,8,128]{3,2,1,0:T(8,128)(2,1)} %bitcast.119), kind=kOutput, calls=%fused_computation.37 | convolution fusion | flops 4295376896 | bytes 100663296 | tf_op jit(solution)/shard_map/rage,ef->ragf/dot_general | solution.py:27
  87.2 62.3 %convert_bitcast_fusion.1 = bf16[4096,4,8,128]{3,2,1,0:T(8,128)(2,1)} fusion(f32[4096,4,8,128]{3,2,1,0:T(8,128)} %fusion.31), kind=kOutput, calls=%fused_computation.16 | convolution fusion | flops 1627390720 | bytes 100663296 | tf_op jit(solution)/shard_map/gh,rahf->ragf/dot_general | solution.py:30
  149.5 49.3 %convert_element_type.82 = bf16[4,8,128,4096]{3,2,1,0:T(8,128)(2,1)} reshape(bf16[4096,4,8,128]{3,2,1,0:T(8,128)(2,1)} %convert_bitcast_fusion.1) | data formatting | bytes 67108864 | tf_op jit(solution)/shard_map/convert_element_type | solution.py:31
  198.8 0.0 copy-start
  198.8 41.4 %copy.36 = bf16[4,8,128,4096]{2,3,1,0:T(8,128)(2,1)} copy(bf16[4,8,128,4096]{3,2,1,0:T(8,128)(2,1)} %convert_element_type.82) | data formatting | bytes 67108864 | tf_op jit(solution)/shard_map/convert_element_type | solution.py:31
  240.1 0.0 copy-done
  240.2 33.2 %convolution_bitcast_fusion.1 = f32[4,8,128,4096]{2,3,1,0:T(8,128)} fusion(bf16[4,8,128,4096]{2,3,1,0:T(8,128)(2,1)} %copy.36, bf16[4,8,128]{2,1,0:T(8,128)(2,1)S(1)} %convert_bitcast_fusion.2), kind=kOutput, calls=%fused_computation.5 | convolution fusion | flops 4312154112 | bytes 100671488 | tf_op jit(solution)/shard_map/ef,cgek->cgfk/dot_general | solution.py:41
  273.4 62.1 %copy.37 = f32[4,8,128,4096]{3,1,2,0:T(8,128)} copy(f32[4,8,128,4096]{2,3,1,0:T(8,128)} %convolution_bitcast_fusion.1) | data formatting | bytes 134217728 | tf_op jit(solution)/shard_map/ef,cgek->cgfk/transpose | solution.py:41
  335.5 63.6 %convert_bitcast_fusion = bf16[4,8,128,4096]{3,1,2,0:T(8,128)(2,1)} fusion(f32[4,8,128,4096]{3,1,2,0:T(8,128)} %copy.37), kind=kOutput, calls=%fused_computation.14 | convolution fusion | flops 1627390720 | bytes 100663296 | tf_op jit(solution)/shard_map/gh,chfk->cgfk/dot_general | solution.py:44
  399.1 29.4 %copy.38 = bf16[4,8,128,4096]{3,2,1,0:T(8,128)(2,1)} copy(bf16[4,8,128,4096]{3,1,2,0:T(8,128)(2,1)} %convert_bitcast_fusion) | data formatting | bytes 67108864 | tf_op jit(solution)/shard_map/convert_element_type | solution.py:45
  428.5 22.7 copy.39
  451.2 7.5 all-to-all-start
  458.7 0.1 fusion.105
  458.8 588.6 %all-to-all-done = bf16[1,4,16,64,4096]{4,3,1,0,2:T(8,128)(2,1)} async-done(((bf16[1,4,16,64,4096]{4,3,1,0,2:T(8,128)(2,1)}), bf16[1,4,16,64,4096]{4,3,1,0,2:T(8,128)(2,1)}, u32[]{:S(2)}, u32[]{:S(2)}) %all-to-all-start) | async-done | bytes 33554464 | tf_op jit(solution)/shard_map/all_to_all | solution.py:77
  1047.4 52.0 %convolution_bitcast_fusion = f32[4,4,4,64,4096]{4,2,0,3,1:T(4,128)} fusion(bf16[4,4,4,64,4096,1]{4,3,2,1,0,5:T(8,128)(2,1)} %bitcast.12, s32[4,4]{1,0:T(4,128)S(1)} %multiply_add_fusion), kind=kOutput, calls=%fused_computation.4 | convolution fusion | flops 536875008 | bytes 100663360 | tf_op jit(solution)/shard_map/sltj,tqjdm->sqldm/dot_general | solution.py:56
  1099.5 83.8 %reshape.67 = f32[4,4,4,64,4,1024]{5,4,2,0,3,1:T(4,128)} reshape(f32[4,4,4,64,4096]{4,2,0,3,1:T(4,128)} %convolution_bitcast_fusion) | data formatting | bytes 134217728 | tf_op jit(solution)/shard_map/reshape | solution.py:59
  1183.2 126.7 %fusion.3 = bf16[4,4,4,64,4,1024]{5,4,1,3,2,0:T(4,128)(2,1)} fusion(f32[4,4,4,64,4,1024]{5,4,2,0,3,1:T(4,128)} %reshape.67, f32[4,4,4,4,1,1,1]{3,1,2,0,6,5,4:T(4,128)S(1)} %fusion.105), kind=kOutput, calls=%fused_computation.6 | convolution fusion | flops 3254779904 | bytes 100664320 | tf_op jit(solution)/shard_map/uvqk,sqldkb->suldvb/dot_general | solution.py:62
  1309.9 23.6 copy.42
  1333.5 53.9 %reshape.68 = bf16[16,4,1,64,4096]{4,3,1,0,2:T(8,128)(2,1)} reshape(bf16[4,4,4,64,4,1024]{5,4,3,2,1,0:T(4,128)(2,1)} %copy.42) | data formatting | bytes 67108864 | tf_op jit(solution)/shard_map/reshape | solution.py:80
  1387.4 0.0 copy-start.1
  1387.4 137.8 %all-to-all-start.1 = ((bf16[16,4,1,64,4096]{4,3,1,2,0:T(8,128)(2,1)}), bf16[16,4,1,64,4096]{4,3,1,2,0:T(8,128)(2,1)}, u32[]{:S(2)}, u32[]{:S(2)}) async-start(bf16[16,4,1,64,4096]{4,3,1,2,0:T(8,128)(2,1)} %bitcast.120), calls=%async_computation.1 | async-start | bytes 67108864 | tf_op jit(solution)/shard_map/all_to_all | solution.py:81
  1525.2 0.0 all-gather.2.cloned.1.call-start
  1525.3 0.7 all-gather.2.cloned.1.call-update
  1526.0 0.0 reduce-scatter.4.cloned.1.call-start
  1526.0 0.0 copy-done.1
  1526.0 638.5 %all-to-all-done.1 = bf16[16,4,1,64,4096]{4,3,1,2,0:T(8,128)(2,1)} async-done(((bf16[16,4,1,64,4096]{4,3,1,2,0:T(8,128)(2,1)}), bf16[16,4,1,64,4096]{4,3,1,2,0:T(8,128)(2,1)}, u32[]{:S(2)}, u32[]{:S(2)}) %all-to-all-start.1) | async-done | bytes 33554464 | tf_op jit(solution)/shard_map/all_to_all | solution.py:81
  2164.5 22.9 copy.44
  2187.4 0.0 all-gather.2.cloned.1.call-done
  2187.4 0.0 copy-start.2
  2187.4 11.3 min.15
  2198.8 11.1 max.15
  2209.9 0.0 copy-done.2
  2209.9 47.8 %fusion.15 = f32[384,4096]{0,1:T(8,128)} fusion(bf16[384,4096]{1,0:T(8,128)(2,1)S(1)} %copy-done.2, bf16[4096,4096]{1,0:T(8,128)(2,1)} %bitcast.124, bf16[512,8,32,128]{3,2,1,0:T(8,128)(2,1)} %bitcast.123, bf16[512,8,32,128]{3,2,1,0:T(8,128)(2,1)} %bitcast.122), kind=kOutput, calls=%fused_computation.19 | convolution fusion | flops 12918456320 | bytes 110100480 | tf_op jit(solution)/shard_map/dot_general | solution.py:88
  2257.7 6.5 copy.58
  2264.3 0.0 reduce-scatter.4.cloned.1.call-update
  2264.3 192.4 %reduce-scatter.4.cloned.1.call-done = f32[96,4096]{1,0:T(8,128)} async-done(((f32[384,4096]{1,0:T(8,128)}), f32[96,4096]{1,0:T(8,128)}) %reduce-scatter.4.cloned.1.call-update) | async-done | bytes 1572880 | tf_op jit(solution)/shard_map/reduce_scatter | solution.py:94
  2456.7 2.4 convert_element_type.91
  (3 shorter events, 0.0 us)
Async XLA Ops:
  198.8 41.4 %copy-start = (s32[4096]{0:T(1024)S(1)}, s32[4096]{0:T(1024)}, u32[]{:S(2)}) copy-start(s32[4096]{0:T(1024)} %param.7) | copy-start | bytes 49156
  451.2 596.2 %all-to-all-start = ((bf16[1,4,16,64,4096]{4,3,1,0,2:T(8,128)(2,1)}), bf16[1,4,16,64,4096]{4,3,1,0,2:T(8,128)(2,1)}, u32[]{:S(2)}, u32[]{:S(2)}) async-start(bf16[1,4,16,64,4096]{4,3,1,0,2:T(8,128)(2,1)} %copy.39), calls=%async_computation | async-start | bytes 67108864 | tf_op jit(solution)/shard_map/all_to_all | solution.py:77
  1387.4 138.6 %copy-start.1 = (s32[32,32]{1,0:T(8,128)S(1)}, s32[32,32]{1,0:T(8,128)}, u32[]{:S(2)}) copy-start(s32[32,32]{1,0:T(8,128)} %param.8) | copy-start | bytes 12292
  1387.4 777.1 %all-to-all-start.1 = ((bf16[16,4,1,64,4096]{4,3,1,2,0:T(8,128)(2,1)}), bf16[16,4,1,64,4096]{4,3,1,2,0:T(8,128)(2,1)}, u32[]{:S(2)}, u32[]{:S(2)}) async-start(bf16[16,4,1,64,4096]{4,3,1,2,0:T(8,128)(2,1)} %bitcast.120), calls=%async_computation.1 | async-start | bytes 67108864 | tf_op jit(solution)/shard_map/all_to_all | solution.py:81
  1525.2 662.2 %all-gather.2.cloned.1.call-start = ((), (), s32[]{:S(2)}) async-start(), calls=%async_computation.3 | async-start | bytes 3932160 | tf_op jit(solution)/shard_map/all_gather | solution.py:89
  1526.0 930.7 %reduce-scatter.4.cloned.1.call-start = ((), (), s32[]{:S(2)}) async-start(), calls=%async_computation.4 | async-start | bytes 7864320 | tf_op jit(solution)/shard_map/reduce_scatter | solution.py:94
  2187.4 22.5 copy-start.2
Sparse Core Ops, SparseCore 0:
  1527.6 258.6 all-gather.1
  2264.4 192.2 reduce-scatter.3
where the time goes:
time: 2480 us; the launch traced here: 2470 us
  waiting for transfers between devices  1420 us (57%)
  local copies, waits for them, and re-layouts  441 us (18%)
  matrix products  419 us (17%)
  starting transfers between devices  145 us (6%)
  other arithmetic  26.5 us (1%)
    all_to_all x1, waiting for transfers between devices, shards(): lax.all_to_all(outgoing, ('row', 'col'), split_axis=0, concat_axis=2, til...  638 us
    all_to_all x1, waiting for transfers between devices, shards(): lax.all_to_all(shaped, ('row', 'col'), split_axis=2, concat_axis=0, tiled...  589 us
    reduce_scatter x1, waiting for transfers between devices, shards(): lax.psum_scatter(partial_out, 'col', scatter_dimension=0, tiled=True)  192 us
    all_to_all x1, starting transfers between devices, shards(): lax.all_to_all(outgoing, ('row', 'col'), split_axis=0, concat_axis=2, til...  138 us
    dot_general x1, matrix products, outer_rotate(): jnp.einsum('uvqk,sqldkb->suldvb', cols_table, spread, precision=lax.Preci...  127 us
    convert_element_type x2, local copies, waits for them, and re-layouts, inner_right(): return mixed.reshape(row_total, col_total).astype(jnp.bfloat16)  90.7 us
    reshape x1, local copies, waits for them, and re-layouts, outer_rotate(): first_mix.reshape(row_count, col_count, out_blocks, first_mix.shape[3], i...  83.8 us
    dot_general x1, matrix products, inner_left(): jnp.einsum('gh,chfk->cgfk', mixing, partial_sum, precision=lax.Precision....  63.6 us
  transfers between devices with their start and end apart: 4, of which 3 were waited for; matrix products, arithmetic and copies ran while one was open for 1% of the time, Pallas kernels for 0%

commit v1 on v0

v1 whole, which is shorter than its diff:
```python
import functools

import jax
import jax.numpy as jnp
from jax import lax
from jax.experimental import pallas as pl
from jax.experimental.pallas import tpu as pltpu
from jax.sharding import PartitionSpec as P

INNER = 1024
D = 16384
BLK = 128
LANES = 128


def sylvester_bf16(length):
    at = jnp.arange(length, dtype=jnp.int32)
    parity = lax.population_count(at[:, None] & at[None, :]) & 1
    return (1 - 2 * parity).astype(jnp.bfloat16)


def inner_kernel(pieces, piece_rows, step, w_ref, si_ref, so_ref, k_ref, out_ref, ws_ref, ks_ref):
    ws_ref[...] = (w_ref[...].astype(jnp.float32) * si_ref[...]).astype(jnp.bfloat16)
    ks_ref[...] = (k_ref[...].astype(jnp.float32) * so_ref[0]).astype(jnp.bfloat16)
    inner = ws_ref.shape[0]

    @pl.loop(0, inner // step)
    def _(n):
        cols = pl.ds(pl.multiple_of(n * step, step), step)
        right = jnp.dot(ws_ref[...], k_ref[:, cols], preferred_element_type=jnp.float32)
        both = jnp.dot(ks_ref[...], right.astype(jnp.bfloat16), preferred_element_type=jnp.float32)
        out_ref[:, 0, :, cols] = both.reshape(pieces, piece_rows, step).astype(jnp.bfloat16)


def inner_both(weight, signs_in, signs_out, table, block, pieces):
    inner = table.shape[0]
    out_blocks = weight.shape[0] // inner
    piece_rows = inner // pieces
    step = min(256, inner)
    return pl.pallas_call(
        functools.partial(inner_kernel, pieces, piece_rows, step),
        grid=(out_blocks,),
        in_specs=[
            pl.BlockSpec((inner, inner), lambda c: (c, block)),
            pl.BlockSpec((1, inner), lambda c: (0, block)),
            pl.BlockSpec((1, 1, inner), lambda c: (c, 0, 0)),
            pl.BlockSpec((inner, inner), lambda c: (0, 0)),
        ],
        out_specs=pl.BlockSpec((pieces, 1, piece_rows, inner), lambda c: (0, c, 0, 0)),
        out_shape=jax.ShapeDtypeStruct((pieces, out_blocks, piece_rows, inner), jnp.bfloat16),
        scratch_shapes=[pltpu.VMEM((inner, inner), jnp.bfloat16)] * 2,
        cost_estimate=pl.CostEstimate(
            flops=4 * out_blocks * inner**3, bytes_accessed=4 * out_blocks * inner**2, transcendentals=0
        ),
    )(weight, signs_in, signs_out, table)


def butterfly(values):
    values = list(values)
    half = 1
    while half < len(values):
        for at in range(len(values)):
            if not at & half:
                low, high = values[at], values[at + half]
                values[at], values[at + half] = low + high, low - high
        half *= 2
    return values


def outer_kernel(row_count, col_count, out_blocks, in_blocks, scale, level_ref, *refs):
    parts = refs[:in_blocks]
    cal_ref, out_ref, mix_ref, clip_ref = refs[in_blocks:]
    b_at, d_at = pl.program_id(0), pl.program_id(1)
    chunk = mix_ref.shape[-1]
    lane_steps = chunk // LANES
    outer_rows = row_count * out_blocks
    outer_cols = col_count * in_blocks
    lane_blocks = level_ref.shape[1] // outer_cols

    @pl.loop(0, col_count * lane_steps)
    def _(at):
        q, lane = at // lane_steps, lax.rem(at, lane_steps)
        cols = pl.ds(pl.multiple_of(lane * LANES, LANES), LANES)
        for k in range(in_blocks):
            mixed = butterfly(
                parts[k][t * col_count + q, j, :, cols].astype(jnp.float32)
                for t in range(row_count)
                for j in range(out_blocks)
            )
            for o in range(outer_rows):
                mix_ref[q * in_blocks + k, o, :, cols] = mixed[o]

    @pl.loop(0, outer_rows * lane_steps)
    def _(at):
        o, lane = at // lane_steps, lax.rem(at, lane_steps)
        cols = pl.ds(pl.multiple_of(lane * LANES, LANES), LANES)
        mixed = butterfly(mix_ref[i, o, :, cols] for i in range(outer_cols))
        for i in range(outer_cols):
            level = level_ref[o, i * lane_blocks + b_at * lane_steps + lane]
            limit = level.astype(jnp.float32) / 512.0
            rotated = mixed[i] * scale
            clip_ref[i, o, :, cols] = jnp.minimum(jnp.maximum(rotated, -limit), limit).astype(jnp.bfloat16)

    total = None
    rows = clip_ref.shape[1] * clip_ref.shape[2]
    for q in range(col_count):
        for k in range(in_blocks):
            cal = cal_ref[:, q, k]
            cal = cal.reshape(cal.shape[0] * cal.shape[1], chunk)
            term = lax.dot_general(
                cal,
                clip_ref[q * in_blocks + k].reshape(rows, chunk),
                (((1,), (1,)), ((), ())),
                preferred_element_type=jnp.float32,
            )
            total = term if total is None else total + term

    @pl.when(b_at == 0)
    def _():
        out_ref[d_at] = total

    @pl.when(b_at > 0)
    def _():
        out_ref[d_at] += total


def outer_project(parts, level, cal, row_count, col_count, scale):
    in_blocks = len(parts)
    pieces, out_blocks, piece_rows, inner = parts[0].shape
    d_block = min(16, piece_rows)
    chunk = min(256, inner)
    outer_rows, outer_cols = row_count * out_blocks, col_count * in_blocks
    cal_local = cal.shape[3]
    cal_rows = row_count * cal_local
    d_steps = piece_rows // d_block
    return pl.pallas_call(
        functools.partial(outer_kernel, row_count, col_count, out_blocks, in_blocks, scale),
        grid=(inner // chunk, d_steps),
        in_specs=[pl.BlockSpec(memory_space=pltpu.SMEM)]
        + [pl.BlockSpec((pieces, out_blocks, d_block, chunk), lambda b, d: (0, 0, d, b))] * in_blocks
        + [pl.BlockSpec((row_count, col_count, in_blocks, cal_local, chunk), lambda b, d: (0, 0, 0, 0, b))],
        out_specs=pl.BlockSpec((d_steps, cal_rows, outer_rows * d_block), lambda b, d: (0, 0, 0)),
        out_shape=jax.ShapeDtypeStruct((d_steps, cal_rows, outer_rows * d_block), jnp.float32),
        scratch_shapes=[
            pltpu.VMEM((outer_cols, outer_rows, d_block, chunk), jnp.float32),
            pltpu.VMEM((outer_cols, outer_rows, d_block, chunk), jnp.bfloat16),
        ],
    )(level, *parts, cal)


def shards(query_weight, sign_input, sign_output, clip_level, calibration):
    rows_local, cols_local = query_weight.shape
    row_count = lax.axis_size("row")
    col_count = lax.axis_size("col")
    pieces = row_count * col_count
    out_blocks = rows_local // INNER
    in_blocks = cols_local // INNER
    piece_rows = INNER // pieces
    cal_local = calibration.shape[0]
    axes = ("row", "col")

    cal = calibration.reshape(cal_local, in_blocks, INNER).transpose(1, 0, 2)
    cal = lax.all_gather(cal, axes, axis=0, tiled=False)
    cal = cal.reshape(row_count, col_count, in_blocks, cal_local, INNER)
    level = lax.all_gather(lax.all_gather(clip_level, "col", axis=1, tiled=True), "row", axis=0, tiled=True)
    place = lax.axis_index("row") * col_count + lax.axis_index("col")
    level = level.reshape(row_count * out_blocks, INNER // BLK, -1)
    level = lax.dynamic_index_in_dim(level, place * piece_rows // BLK, axis=1, keepdims=False)

    table = sylvester_bf16(INNER)
    signs_in = sign_input.astype(jnp.float32).reshape(1, cols_local)
    signs_out = sign_output.astype(jnp.float32).reshape(out_blocks, 1, INNER)
    parts = []
    for block in range(in_blocks):
        tile = inner_both(query_weight, signs_in, signs_out, table, block, pieces)
        parts.append(lax.all_to_all(tile, axes, split_axis=0, concat_axis=0, tiled=True))

    total = outer_project(parts, level, cal, row_count, col_count, 1.0 / D)
    d_steps, cal_rows = total.shape[:2]
    d_block = piece_rows // d_steps
    result = total.astype(jnp.bfloat16)
    result = result.reshape(d_steps, col_count, cal_rows // col_count, row_count, out_blocks, d_block)
    result = result.transpose(3, 1, 2, 4, 0, 5)
    result = result.reshape(pieces, cal_rows // col_count, out_blocks, piece_rows)
    result = lax.all_to_all(result, axes, split_axis=0, concat_axis=0, tiled=True)
    return result.transpose(1, 2, 0, 3).reshape(cal_rows // col_count, rows_local)


def solution(mesh):
    placed = (
        P(("layer", "row"), "col"),
        P(("layer", "col")),
        P(("layer", "row")),
        P(("layer", "row"), "col"),
        P(("layer", "row"), "col"),
    )
    return jax.shard_map(
        shards, mesh=mesh, in_specs=placed, out_specs=P(("layer", "col"), "row"), check_vma=False
    )
```

time: 2480 us -> 998 us (0.40)
  waiting for transfers between devices: 1420 us -> 398 us
  local copies, waits for them, and re-layouts: 441 us -> 4.98 us
  matrix products: 419 us -> 0 us
  Pallas kernels: 0 us -> 238 us
  blocking collectives: 0 us -> 219 us
  starting transfers between devices: 145 us -> 117 us
    all_to_all x2 -> x4, waiting for transfers between devices: 1230 us -> 398 us  [shards(): lax.all_to_all(tile, axes, split_axis=0, concat_axis=0, tiled=True)]
    dot_general x7 -> x0, matrix products: 419 us -> none  [the longest x1 127 us: outer_rotate(): jnp.einsum('uvqk,sqldkb->suldvb', cols_table, spread, precision=lax.Preci...]
    pallas_call x0 -> x5, Pallas kernels: none -> 238 us  [the longest x4 171 us: inner_both(): pl.pallas_call(functools.partial(inner_kernel, pieces, piece_rows, step),...]
    reduce_scatter x1 -> x0, waiting for transfers between devices: 192 us -> none  [shards(): lax.psum_scatter(partial_out, 'col', scatter_dimension=0, tiled=True)]
    all_gather x0 -> x2, blocking collectives: none -> 189 us  [the longest x1 151 us: shards(): lax.all_gather(lax.all_gather(clip_level, 'col', axis=1, tiled=True), 'ro...]
    convert_element_type x5 -> x1, local copies, waits for them, and re-layouts: 166 us -> 0.36 us  [shards(): result = total.astype(jnp.bfloat16)]
    reshape x2 -> x3, local copies, waits for them, and re-layouts: 138 us -> 2.43 us  [the longest x1 1.25 us: shards(): result.transpose(1, 2, 0, 3).reshape(cal_rows // col_count, rows_local)]
    transpose x1 -> x3, local copies, waits for them, and re-layouts: 62.1 us -> 1.45 us  [the longest x1 1.12 us: shards(): cal = calibration.reshape(cal_local, in_blocks, INNER).transpose(1, 0, 2)]
  transfers between devices with their start and end apart: 4 -> 5, of which waited for: 3 -> 3; matrix products, arithmetic and copies ran while one was open for 1% -> 0% of each run, Pallas kernels for 0% -> 13%
where the time goes in v1:
time: 998 us; the launch traced here: 996 us
  waiting for transfers between devices  398 us (40%)
  Pallas kernels  238 us (24%)
  blocking collectives  219 us (22%)
  starting transfers between devices  117 us (12%)
  between operations  13.5 us (1%)
    all_to_all x4, waiting for transfers between devices, shards(): lax.all_to_all(tile, axes, split_axis=0, concat_axis=0, tiled=True)  398 us
    pallas_call x4, Pallas kernels, inner_both(): pl.pallas_call(functools.partial(inner_kernel, pieces, piece_rows, step),...  171 us
    all_gather x1, blocking collectives, shards(): lax.all_gather(lax.all_gather(clip_level, 'col', axis=1, tiled=True), 'ro...  151 us
    all_to_all x4, starting transfers between devices, shards(): lax.all_to_all(tile, axes, split_axis=0, concat_axis=0, tiled=True)  117 us
    pallas_call x1, Pallas kernels, outer_project(): pl.pallas_call(functools.partial(outer_kernel, row_count, col_count, out_...  67.1 us
    all_gather x1, blocking collectives, shards(): lax.all_gather(clip_level, 'col', axis=1, tiled=True)  38.9 us
    all_to_all x1, blocking collectives, shards(): lax.all_to_all(result, axes, split_axis=0, concat_axis=0, tiled=True)  29.2 us
  transfers between devices with their start and end apart: 5, of which 3 were waited for; matrix products, arithmetic and copies ran while one was open for 0% of the time, Pallas kernels for 13%

profile of v1, /device:TPU:0, one launch (start us, length us, event | category | flops | bytes accessed | tf_op | source)
XLA Modules:
  0.0 996.4 jit_solution(11558885438403139765)
XLA Ops:
  6.5 2.5 subtract_convert_fusion.k_ref
  9.0 1.3 convert_element_type.18
  10.4 1.3 convert_element_type.19
  11.7 42.7 %shard_map.55 = bf16[16,4,64,1024]{3,2,1,0:T(8,128)(2,1)} custom-call(bf16[4096,4096]{1,0:T(8,128)(2,1)} %w_ref.7, f32[1,4096]{1,0:T(1,128)} %bitcast.20, f32[4,1,1024]{2,1,0:T(1,128)} %bitcast.24, bf16[1024,1024]{1,0:T(8,128)(2,1)} %subtract_convert_fusion.k_ref), custom_call_target="tpu_custom_call" | custom-call | flops 17179869184 | bytes 16777216 | tf_op jit(solution)/shard_map/pallas_call | solution.py:40
  54.4 7.5 all-to-all-start
  61.9 42.8 %shard_map.56 = bf16[16,4,64,1024]{3,2,1,0:T(8,128)(2,1)} custom-call(bf16[4096,4096]{1,0:T(8,128)(2,1)} %w_ref.7, f32[1,4096]{1,0:T(1,128)} %bitcast.21, f32[4,1,1024]{2,1,0:T(1,128)} %bitcast.25, bf16[1024,1024]{1,0:T(8,128)(2,1)} %subtract_convert_fusion.k_ref), custom_call_target="tpu_custom_call" | custom-call | flops 17179869184 | bytes 16777216 | tf_op jit(solution)/shard_map/pallas_call | solution.py:40
  104.7 107.7 %all-to-all-done.refs_0_ = bf16[16,4,64,1024]{3,2,1,0:T(8,128)(2,1)} async-done(((bf16[16,4,64,1024]{3,2,1,0:T(8,128)(2,1)}), bf16[16,4,64,1024]{3,2,1,0:T(8,128)(2,1)}, u32[]{:S(2)}, u32[]{:S(2)}) %all-to-all-start) | async-done | bytes 8388640 | tf_op jit(solution)/shard_map/all_to_all | solution.py:176
  212.4 36.5 %all-to-all-start.1 = ((bf16[16,4,64,1024]{3,2,1,0:T(8,128)(2,1)}), bf16[16,4,64,1024]{3,2,1,0:T(8,128)(2,1)}, u32[]{:S(2)}, u32[]{:S(2)}) async-start(bf16[16,4,64,1024]{3,2,1,0:T(8,128)(2,1)} %shard_map.56), calls=%async_computation.1 | async-start | bytes 16777216 | tf_op jit(solution)/shard_map/all_to_all | solution.py:176
  249.0 42.7 %shard_map.57 = bf16[16,4,64,1024]{3,2,1,0:T(8,128)(2,1)} custom-call(bf16[4096,4096]{1,0:T(8,128)(2,1)} %w_ref.7, f32[1,4096]{1,0:T(1,128)} %bitcast.22, f32[4,1,1024]{2,1,0:T(1,128)} %bitcast.26, bf16[1024,1024]{1,0:T(8,128)(2,1)} %subtract_convert_fusion.k_ref), custom_call_target="tpu_custom_call" | custom-call | flops 17179869184 | bytes 16777216 | tf_op jit(solution)/shard_map/pallas_call | solution.py:40
  291.7 0.0 copy-start
  291.7 107.8 %all-to-all-done.1.refs_1_ = bf16[16,4,64,1024]{3,2,1,0:T(8,128)(2,1)} async-done(((bf16[16,4,64,1024]{3,2,1,0:T(8,128)(2,1)}), bf16[16,4,64,1024]{3,2,1,0:T(8,128)(2,1)}, u32[]{:S(2)}, u32[]{:S(2)}) %all-to-all-start.1) | async-done | bytes 8388640 | tf_op jit(solution)/shard_map/all_to_all | solution.py:176
  399.6 36.5 %all-to-all-start.2 = ((bf16[16,4,64,1024]{3,2,1,0:T(8,128)(2,1)}), bf16[16,4,64,1024]{3,2,1,0:T(8,128)(2,1)}, u32[]{:S(2)}, u32[]{:S(2)}) async-start(bf16[16,4,64,1024]{3,2,1,0:T(8,128)(2,1)} %shard_map.57), calls=%async_computation.2 | async-start | bytes 16777216 | tf_op jit(solution)/shard_map/all_to_all | solution.py:176
  436.1 0.0 all-gather.3.cloned.1.call-start
  436.2 0.0 copy-done
  436.2 0.6 reshape.27
  436.8 1.1 copy.22
  437.9 0.0 all-gather.3.cloned.1.call-update
  437.9 42.8 %shard_map.58 = bf16[16,4,64,1024]{3,2,1,0:T(8,128)(2,1)} custom-call(bf16[4096,4096]{1,0:T(8,128)(2,1)} %w_ref.7, f32[1,4096]{1,0:T(1,128)} %bitcast.23, f32[4,1,1024]{2,1,0:T(1,128)} %bitcast.27, bf16[1024,1024]{1,0:T(8,128)(2,1)} %subtract_convert_fusion.k_ref), custom_call_target="tpu_custom_call" | custom-call | flops 17179869184 | bytes 16777216 | tf_op jit(solution)/shard_map/pallas_call | solution.py:40
  480.6 0.0 copy-start.1
  480.6 181.9 %all-to-all-done.2.refs_2_ = bf16[16,4,64,1024]{3,2,1,0:T(8,128)(2,1)} async-done(((bf16[16,4,64,1024]{3,2,1,0:T(8,128)(2,1)}), bf16[16,4,64,1024]{3,2,1,0:T(8,128)(2,1)}, u32[]{:S(2)}, u32[]{:S(2)}) %all-to-all-start.2) | async-done | bytes 8388640 | tf_op jit(solution)/shard_map/all_to_all | solution.py:176
  662.6 36.5 %all-to-all-start.3 = ((bf16[16,4,64,1024]{3,2,1,0:T(8,128)(2,1)}), bf16[16,4,64,1024]{3,2,1,0:T(8,128)(2,1)}, u32[]{:S(2)}, u32[]{:S(2)}) async-start(bf16[16,4,64,1024]{3,2,1,0:T(8,128)(2,1)} %shard_map.58), calls=%async_computation.3 | async-start | bytes 16777216 | tf_op jit(solution)/shard_map/all_to_all | solution.py:176
  699.1 0.0 copy-done.1
  699.1 0.1 copy.20
  699.1 38.9 %all_gather.12 = s32[32,128]{0,1:T(8,128)S(1)} all-gather(s32[32,32]{0,1:T(8,128)S(1)} %copy.20), channel_id=1, replica_groups=mesh['layer'=2,'row'=4,'col'=4] {'col'}, dimensions={1}, use_global_device_ids=true | all-gather | bytes 20480 | tf_op jit(solution)/shard_map/all_gather | solution.py:165
  738.0 0.1 copy.21
  738.1 150.5 %all_gather.13 = s32[128,128]{1,0:T(8,128)S(1)} all-gather(s32[32,128]{1,0:T(8,128)S(1)} %copy.21), channel_id=1, replica_groups=mesh['layer'=2,'row'=4,'col'=4] {'row'}, dimensions={0}, use_global_device_ids=true | all-gather | bytes 81920 | tf_op jit(solution)/shard_map/all_gather | solution.py:165
  888.6 0.6 constant_dynamic-slice_fusion
  889.2 0.0 all-to-all-done.3.refs_3_
  889.2 0.0 all-gather.3.cloned.1.call-done
  889.2 67.1 %shard_map.59 = f32[4,384,256]{2,1,0:T(8,128)} custom-call(s32[16,128]{1,0:T(8,128)} %bitcast.19, bf16[16,4,64,1024]{3,2,1,0:T(8,128)(2,1)} %all-to-all-done.refs_0_, bf16[16,4,64,1024]{3,2,1,0:T(8,128)(2,1)} %all-to-all-done.1.refs_1_, bf16[16,4,64,1024]{3,2,1,0:T(8,128)(2,1)} %all-to-all-done.2.refs_2_, bf16[16,4,64,1024]{3,2,1,0:T(8,128)(2,1)} %all-to-all-done.3.refs_3_, ...), custom_call_target="tpu_custom_call" | custom-call | tf_op jit(solution)/shard_map/pallas_call | solution.py:136
  956.3 1.5 convert_element_type.21
  957.8 0.4 copy.23
  958.2 0.6 reshape.29
  958.8 0.3 copy.24
  959.1 29.2 %all_to_all.25 = bf16[16,96,4,64]{1,3,2,0:T(8,128)(2,1)S(1)} all-to-all(bf16[16,96,4,64]{1,3,2,0:T(8,128)(2,1)S(1)} %bitcast.15), channel_id=1, replica_groups=mesh['layer'=2,'row'=4,'col'=4] {'row','col'}, dimensions={0} | all-to-all | bytes 1572864 | tf_op jit(solution)/shard_map/all_to_all | solution.py:185
  988.2 0.1 copy.25
  988.3 1.2 copy.26
Async XLA Ops:
  54.4 158.0 %all-to-all-start = ((bf16[16,4,64,1024]{3,2,1,0:T(8,128)(2,1)}), bf16[16,4,64,1024]{3,2,1,0:T(8,128)(2,1)}, u32[]{:S(2)}, u32[]{:S(2)}) async-start(bf16[16,4,64,1024]{3,2,1,0:T(8,128)(2,1)} %shard_map.55), calls=%async_computation | async-start | bytes 16777216 | tf_op jit(solution)/shard_map/all_to_all | solution.py:176
  212.4 187.1 %all-to-all-start.1 = ((bf16[16,4,64,1024]{3,2,1,0:T(8,128)(2,1)}), bf16[16,4,64,1024]{3,2,1,0:T(8,128)(2,1)}, u32[]{:S(2)}, u32[]{:S(2)}) async-start(bf16[16,4,64,1024]{3,2,1,0:T(8,128)(2,1)} %shard_map.56), calls=%async_computation.1 | async-start | bytes 16777216 | tf_op jit(solution)/shard_map/all_to_all | solution.py:176
  291.7 144.4 %copy-start = (bf16[96,4096]{1,0:T(8,128)(2,1)S(1)}, bf16[96,4096]{1,0:T(8,128)(2,1)}, u32[]{:S(2)}) copy-start(bf16[96,4096]{1,0:T(8,128)(2,1)} %param.9) | copy-start | bytes 2359300
  399.6 263.0 %all-to-all-start.2 = ((bf16[16,4,64,1024]{3,2,1,0:T(8,128)(2,1)}), bf16[16,4,64,1024]{3,2,1,0:T(8,128)(2,1)}, u32[]{:S(2)}, u32[]{:S(2)}) async-start(bf16[16,4,64,1024]{3,2,1,0:T(8,128)(2,1)} %shard_map.57), calls=%async_computation.2 | async-start | bytes 16777216 | tf_op jit(solution)/shard_map/all_to_all | solution.py:176
  436.1 453.1 %all-gather.3.cloned.1.call-start = ((), (), s32[]{:S(2)}) async-start(), calls=%async_computation.5 | async-start | bytes 13369344 | tf_op jit(solution)/shard_map/all_gather | solution.py:163
  480.6 218.4 %copy-start.1 = (s32[32,32]{1,0:T(8,128)S(1)}, s32[32,32]{1,0:T(8,128)}, u32[]{:S(2)}) copy-start(s32[32,32]{1,0:T(8,128)} %param.8) | copy-start | bytes 12292
  662.6 226.7 %all-to-all-start.3 = ((bf16[16,4,64,1024]{3,2,1,0:T(8,128)(2,1)}), bf16[16,4,64,1024]{3,2,1,0:T(8,128)(2,1)}, u32[]{:S(2)}, u32[]{:S(2)}) async-start(bf16[16,4,64,1024]{3,2,1,0:T(8,128)(2,1)} %shard_map.58), calls=%async_computation.3 | async-start | bytes 16777216 | tf_op jit(solution)/shard_map/all_to_all | solution.py:176
Sparse Core Ops, SparseCore 0:
  439.2 217.5 all-gather.2
